TPU v7x, 512 devices: a whole 4x4x16 slice. The times are simulated.
512 devices in a mesh: vocab: 64 (over z, x), dp: 8 (over y, core).
Axes of the slice: x: 4, y: 4, z: 16, core: 2. Of those that a mesh axis runs over, the one named last changes fastest.
Arguments:
- hidden_states: bfloat16 [8192, 3584], P(('dp', 'vocab')), parts along dimension 0
- final_gain: float32 [3584], replicated, may hold values from 0.1 to 1.9
- head_weight: bfloat16 [3584, 40960], P(None, 'vocab')
- targets: int32 [8192], P('dp'), parts along dimension 0, may hold values from 0 to 40959
- lengths: int32 [128], P('dp'), parts along dimension 0, may hold values from 1 to 64, 640 in all
- slot_mask: int32 [8192], P(('dp', 'vocab')), parts along dimension 0, may hold values 0 or 1
Outputs:
- logprob: float32 [8192], P(('dp', 'vocab')), parts along dimension 0
- entropy: float32 [8192], P(('dp', 'vocab')), parts along dimension 0
There are 8 independent parts, one for each index of `dp`. A program takes and returns all parts, laid end to end along the dimension named above; an argument that names none is the same for every part. Nothing has to cross between parts.
Inputs may be any that keep to these rules, and one draw needn't show every extreme that they name: Sequence s owns slots s * 64 to (s + 1) * 64 - 1; its first lengths[s] slots are responses, and one sequence fills all 64.
All inputs are finite; a program needn't handle non-finite values. No bound on the sum of `slot_mask` on one device may be relied on, other than what follows from the above.
Results may differ from a plain program's by a relative error of at most 0.0003.
The roundings to bfloat16 on the way count: a program that leaves them out, or rounds other values in their place, can miss the bound.
Values may be sent and summed in bfloat16 or wider, within the bound.
No kernel may reach another device: no remote copies, remote signals or barrier semaphores. Data moves between devices by JAX's collectives and lax.ppermute only.
A program may use at most 64 MiB of HBM per device.

v0:
```python
import jax
import jax.numpy as jnp
from jax import lax
from jax.sharding import PartitionSpec as P

SLOT_LEN = 64


def normalize(block, final_gain):
    values = block.astype(jnp.float32)
    square_mean = jnp.mean(values * values, axis=-1, keepdims=True)
    return (values * lax.rsqrt(square_mean + 1e-05) * final_gain).astype(jnp.bfloat16)


def row_stats(normed_rows, head_weight, targets, columns):
    logits = jnp.dot(normed_rows, head_weight, preferred_element_type=jnp.float32)
    highest = jnp.max(logits, axis=1)
    shifted = jnp.exp(logits - highest[:, None])
    total = jnp.sum(shifted, axis=1)
    weighted = jnp.sum(shifted * logits, axis=1)
    chosen = jnp.sum(jnp.where(columns[None, :] == targets[:, None], logits, 0.0), axis=1)
    return jnp.stack([highest, total, weighted, chosen], axis=0)


def body(hidden_states, final_gain, head_weight, targets, lengths, slot_mask):
    tok_dev = hidden_states.shape[0]
    v_dev = head_weight.shape[1]
    columns = lax.axis_index("vocab") * v_dev + jnp.arange(v_dev, dtype=jnp.int32)
    normed = normalize(hidden_states, final_gain)
    stats = row_stats(
        lax.all_gather(normed, "vocab", axis=0, tiled=True), head_weight, targets, columns
    )
    highest, total, weighted, chosen = (stats[0], stats[1], stats[2], stats[3])
    offset = lax.axis_index("vocab") * tok_dev
    overall = lax.pmax(highest, "vocab")
    factor = jnp.exp(highest - overall)
    total, weighted, chosen = lax.psum((total * factor, weighted * factor, chosen), "vocab")
    own_peak = lax.dynamic_slice_in_dim(overall, offset, tok_dev)
    own_total = lax.dynamic_slice_in_dim(total, offset, tok_dev)
    own_weighted = lax.dynamic_slice_in_dim(weighted, offset, tok_dev)
    own_chosen = lax.dynamic_slice_in_dim(chosen, offset, tok_dev)
    slot_index = offset + jnp.arange(tok_dev, dtype=jnp.int32)
    sequence = slot_index // SLOT_LEN
    seq_ids = jnp.arange(lengths.shape[0], dtype=jnp.int32)
    length_of = jnp.sum(
        jnp.where(sequence[:, None] == seq_ids[None, :], lengths[None, :], 0), axis=1
    )
    valid = jnp.logical_and(slot_index % SLOT_LEN < length_of, slot_mask == 1)
    log_total = jnp.log(own_total)
    logprob = jnp.where(valid, own_chosen - own_peak - log_total, jnp.float32(0.0))
    entropy = jnp.where(valid, own_peak + log_total - own_weighted / own_total, jnp.float32(0.0))
    return (logprob, entropy)


def solution(mesh):
    in_specs = (
        P(("dp", "vocab"), None),
        P(),
        P(None, "vocab"),
        P("dp"),
        P("dp"),
        P(("dp", "vocab")),
    )
    out_specs = (P(("dp", "vocab")), P(("dp", "vocab")))
    return jax.shard_map(body, mesh=mesh, in_specs=in_specs, out_specs=out_specs, check_vma=False)
```

profile of v0, /device:TPU:16, one launch (start us, length us, event | category | flops | bytes accessed | tf_op | source)
XLA Modules:
  0.0 600.2 jit_solution(14900941998563830935)
XLA Ops:
  7.2 0.0 all-gather.2.cloned.1.call-start
  7.2 1.0 fusion.1
  8.3 1.6 fusion.3
  9.9 0.0 all-gather.2.cloned.1.call-update
  10.0 0.8 select_reduce_fusion.1
  10.8 0.0 copy-start
  10.8 157.4 %all-gather.2.cloned.1.call-done = bf16[1024,3584]{1,0:T(8,128)(2,1)} async-done(((bf16[16,3584]{1,0:T(8,128)(2,1)}), bf16[1024,3584]{1,0:T(8,128)(2,1)}) %all-gather.2.cloned.1.call-update) | async-done | bytes 7340048 | tf_op jit(solution)/shard_map/all_gather | solution.py:31
  168.2 8.6 %fusion.6 = (f32[1024]{0:T(1024)S(1)}, f32[1024,640]{0,1:T(8,128)S(1)}) fusion(bf16[1024,3584]{1,0:T(8,128)(2,1)} %all-gather.2.cloned.1.call-done, bf16[3584,640]{1,0:T(8,128)(2,1)} %param.8), kind=kOutput, calls=%fused_computation.25 | convolution fusion | flops 4698274816 | bytes 14553088 | tf_op jit(solution)/shard_map/dot_general | solution.py:16
  176.8 0.0 copy-start.1
  176.8 141.1 %pmax.7 = f32[1024]{0:T(1024)S(1)} all-reduce(f32[1024]{0:T(1024)S(1)} %get-tuple-element.12), channel_id=1, replica_groups=mesh['vocab'=64,'dp'=8] {'vocab'}, use_global_device_ids=true, to_apply=%region_5.6 | all-reduce | flops 1024 | bytes 8192 | tf_op jit(solution)/shard_map/pmax | solution.py:35
  318.0 0.0 copy-done
  318.0 0.8 multiply_reduce_fusion
  318.8 274.0 %all-reduce = (f32[1024]{0:T(1024)S(1)}, f32[1024]{0:T(1024)S(1)}, f32[1024]{0:T(1024)S(1)}) all-reduce(f32[1024]{0:T(1024)S(1)} %get-tuple-element.4, f32[1024]{0:T(1024)S(1)} %get-tuple-element.11, f32[1024]{0:T(1024)S(1)} %get-tuple-element.10), channel_id=1, replica_groups=mesh['vocab'=64,'dp'=8] {'vocab'}, use_global_device_ids=true, to_apply=%region_3.0 | all-reduce | flops 3072 | bytes 24576 | tf_op jit(solution)/shard_map/psum | solution.py:37
  592.8 0.0 copy-done.1
  592.8 0.6 subtract_select_fusion
  (4 shorter events, 0.0 us)
Async XLA Ops:
  7.2 161.0 %all-gather.2.cloned.1.call-start = ((), (), s32[]{:S(2)}) async-start(), calls=%async_computation | async-start | bytes 7454720 | tf_op jit(solution)/shard_map/all_gather | solution.py:31
  10.8 307.2 %copy-start = (s32[1024]{0:T(1024)S(1)}, s32[1024]{0:T(1024)}, u32[]{:S(2)}) copy-start(s32[1024]{0:T(1024)} %param.9) | copy-start | bytes 12292
  176.8 415.9 %copy-start.1 = (s32[16]{0:T(128)S(1)}, s32[16]{0:T(128)}, u32[]{:S(2)}) copy-start(s32[16]{0:T(128)} %param.11) | copy-start | bytes 196
Sparse Core Ops, SparseCore 0:
  10.9 157.2 all-gather.1
where the time goes:
time: 600 us
  blocking collectives  415 us (69%)
  waiting for transfers between devices  157 us (26%)
  between operations  14.1 us (2%)
  matrix products  8.63 us (1%)
    psum x1, blocking collectives, body(): lax.psum((total * factor, weighted * factor, chosen), 'vocab')  274 us
    all_gather x1, waiting for transfers between devices, body(): lax.all_gather(normed, 'vocab', axis=0, tiled=True)  157 us
    pmax x1, blocking collectives, body(): overall = lax.pmax(highest, 'vocab')  141 us
  transfers between devices with their start and end apart: 1, of which 1 were waited for; matrix products, arithmetic and copies ran while one was open for 0% of the time, Pallas kernels for 0%

commit v1 on v0

--- a/solution.py
+++ b/solution.py
@@ -4,6 +4,7 @@
 from jax.sharding import PartitionSpec as P
 
 SLOT_LEN = 64
+RING = 4
 
 
 def normalize(block, final_gain):
@@ -22,23 +23,36 @@
     return jnp.stack([highest, total, weighted, chosen], axis=0)
 
 
-def body(hidden_states, final_gain, head_weight, targets, lengths, slot_mask):
+def gather_rows(normed, n_vocab):
+    near = [[z * RING + x for x in range(RING)] for z in range(n_vocab // RING)]
+    far = [[z * RING + x for z in range(n_vocab // RING)] for x in range(RING)]
+    rows = lax.all_gather(normed, "vocab", axis=0, tiled=True, axis_index_groups=near)
+    return lax.all_gather(rows, "vocab", axis=0, tiled=True, axis_index_groups=far)
+
+
+def exchange(stats, n_vocab):
+    own = stats.shape[1] // n_vocab
+    sent = stats.reshape(4, n_vocab, own).transpose(1, 0, 2).reshape(n_vocab, 4 * own)
+    got = lax.all_to_all(sent, "vocab", 0, 0, tiled=True).reshape(n_vocab, 4, own)
+    highest, total, weighted, chosen = got[:, 0], got[:, 1], got[:, 2], got[:, 3]
+    peak = jnp.max(highest, axis=0)
+    factor = jnp.exp(highest - peak)
+    return (
+        peak,
+        jnp.sum(total * factor, axis=0),
+        jnp.sum(weighted * factor, axis=0),
+        jnp.sum(chosen, axis=0),
+    )
+
+
+def body(n_vocab, hidden_states, final_gain, head_weight, targets, lengths, slot_mask):
     tok_dev = hidden_states.shape[0]
     v_dev = head_weight.shape[1]
     columns = lax.axis_index("vocab") * v_dev + jnp.arange(v_dev, dtype=jnp.int32)
     normed = normalize(hidden_states, final_gain)
-    stats = row_stats(
-        lax.all_gather(normed, "vocab", axis=0, tiled=True), head_weight, targets, columns
-    )
-    highest, total, weighted, chosen = (stats[0], stats[1], stats[2], stats[3])
+    stats = row_stats(gather_rows(normed, n_vocab), head_weight, targets, columns)
+    own_peak, own_total, own_weighted, own_chosen = exchange(stats, n_vocab)
     offset = lax.axis_index("vocab") * tok_dev
-    overall = lax.pmax(highest, "vocab")
-    factor = jnp.exp(highest - overall)
-    total, weighted, chosen = lax.psum((total * factor, weighted * factor, chosen), "vocab")
-    own_peak = lax.dynamic_slice_in_dim(overall, offset, tok_dev)
-    own_total = lax.dynamic_slice_in_dim(total, offset, tok_dev)
-    own_weighted = lax.dynamic_slice_in_dim(weighted, offset, tok_dev)
-    own_chosen = lax.dynamic_slice_in_dim(chosen, offset, tok_dev)
     slot_index = offset + jnp.arange(tok_dev, dtype=jnp.int32)
     sequence = slot_index // SLOT_LEN
     seq_ids = jnp.arange(lengths.shape[0], dtype=jnp.int32)
@@ -53,6 +67,7 @@
 
 
 def solution(mesh):
+    n_vocab = mesh.shape["vocab"]
     in_specs = (
         P(("dp", "vocab"), None),
         P(),
@@ -62,4 +77,8 @@
         P(("dp", "vocab")),
     )
     out_specs = (P(("dp", "vocab")), P(("dp", "vocab")))
-    return jax.shard_map(body, mesh=mesh, in_specs=in_specs, out_specs=out_specs, check_vma=False)
+
+    def run(*args):
+        return body(n_vocab, *args)
+
+    return jax.shard_map(run, mesh=mesh, in_specs=in_specs, out_specs=out_specs, check_vma=False)

time: 600 us -> 169 us (0.28)
  the two profiles are of different devices: /device:TPU:16 before, /device:TPU:8 now
where the time goes in v1:
time: 169 us
  waiting for transfers between devices  114 us (67%)
  between operations  14.1 us (8%)
  blocking collectives  13.7 us (8%)
  starting transfers between devices  12.2 us (7%)
  matrix products  8.63 us (5%)
  other arithmetic  4.4 us (3%)
    all_gather x1, waiting for transfers between devices, gather_rows(): lax.all_gather(rows, 'vocab', axis=0, tiled=True, axis_index_groups=far)  99.8 us
    all_to_all x1, waiting for transfers between devices, exchange(): lax.all_to_all(sent, 'vocab', 0, 0, tiled=True).reshape(n_vocab, 4, own)  14.6 us
    all_gather x1, blocking collectives, gather_rows(): lax.all_gather(normed, 'vocab', axis=0, tiled=True, axis_index_groups=near)  13.7 us
    all_to_all x1, starting transfers between devices, exchange(): lax.all_to_all(sent, 'vocab', 0, 0, tiled=True).reshape(n_vocab, 4, own)  12.2 us
    dot_general x1, matrix products, row_stats(): jnp.dot(normed_rows, head_weight, preferred_element_type=jnp.float32)  8.63 us
  transfers between devices with their start and end apart: 2, of which 2 were waited for; matrix products, arithmetic and copies ran while one was open for 0% of the time, Pallas kernels for 0%

profile of v1, /device:TPU:8, one launch (start us, length us, event | category | flops | bytes accessed | tf_op | source)
XLA Modules:
  0.0 168.9 jit_solution(7229137232615458997)
XLA Ops:
  7.2 0.0 all-gather.2.cloned.1.call-start
  7.2 1.0 fusion.1
  8.3 1.0 fusion.3
  9.3 13.7 %all_gather.6 = bf16[64,3584]{1,0:T(8,128)(2,1)} all-gather(bf16[16,3584]{1,0:T(8,128)(2,1)S(1)} %fusion.3), channel_id=1, replica_groups={{0,8,16,24},{32,40,48,56},{64,72,80,88},{96,104,112,120},{128,136,144,1..., dimensions={0}, use_global_device_ids=true | all-gather | bytes 573440 | tf_op jit(solution)/shard_map/all_gather | solution.py:29
  23.0 0.0 all-gather.2.cloned.1.call-update
  23.1 0.0 copy-start
  23.1 99.8 %all-gather.2.cloned.1.call-done = bf16[1024,3584]{1,0:T(8,128)(2,1)} async-done(((bf16[64,3584]{1,0:T(8,128)(2,1)}), bf16[1024,3584]{1,0:T(8,128)(2,1)}) %all-gather.2.cloned.1.call-update) | async-done | bytes 7340048 | tf_op jit(solution)/shard_map/all_gather | solution.py:30
  122.9 8.6 %fusion.9 = (f32[1024]{0:T(1024)S(1)}, f32[1024,640]{0,1:T(8,128)S(1)}) fusion(bf16[1024,3584]{1,0:T(8,128)(2,1)} %all-gather.2.cloned.1.call-done, bf16[3584,640]{1,0:T(8,128)(2,1)} %param.8), kind=kOutput, calls=%fused_computation.33 | convolution fusion | flops 4698274816 | bytes 14553088 | tf_op jit(solution)/shard_map/dot_general | solution.py:17
  131.5 0.0 copy-start.2
  131.5 0.0 copy-start.1
  131.5 0.1 stack.15
  131.6 0.0 copy-done
  131.6 0.8 fusion
  132.4 0.1 stack.16
  132.5 0.1 copy.18
  132.5 0.1 stack.17
  132.6 0.1 copy.19
  132.7 0.1 stack.18
  132.8 0.1 copy.20
  132.8 0.1 copy.17
  132.9 0.7 copy.21
  133.6 12.2 %all-to-all-start = ((f32[64,1,64]{2,1,0:T(1,128)}), f32[64,1,64]{2,1,0:T(1,128)S(1)}, u32[]{:S(2)}, u32[]{:S(2)}) async-start(f32[64,1,64]{2,1,0:T(1,128)} %copy.21), calls=%async_computation | async-start | bytes 65536 | tf_op jit(solution)/shard_map/all_to_all | solution.py:36
  145.8 0.0 copy-done.2
  145.8 0.2 select_reduce_fusion.1
  146.0 14.6 %all-to-all-done = f32[64,1,64]{2,1,0:T(1,128)S(1)} async-done(((f32[64,1,64]{2,1,0:T(1,128)}), f32[64,1,64]{2,1,0:T(1,128)S(1)}, u32[]{:S(2)}, u32[]{:S(2)}) %all-to-all-start) | async-done | bytes 16416 | tf_op jit(solution)/shard_map/all_to_all | solution.py:36
  160.6 0.1 copy.22
  160.7 0.1 slice_reduce_fusion.1
  160.8 0.2 fusion.5
  161.0 0.0 copy-done.1
  161.0 0.5 subtract_select_fusion
  161.5 0.5 subtract_select_fusion.1
  (4 shorter events, 0.0 us)
Async XLA Ops:
  7.2 115.7 %all-gather.2.cloned.1.call-start = ((), (), s32[]{:S(2)}) async-start(), calls=%async_computation.1 | async-start | bytes 7798784 | tf_op jit(solution)/shard_map/all_gather | solution.py:30
  23.1 108.5 %copy-start = (s32[1024]{0:T(1024)S(1)}, s32[1024]{0:T(1024)}, u32[]{:S(2)}) copy-start(s32[1024]{0:T(1024)} %param.9) | copy-start | bytes 12292
  131.5 14.3 %copy-start.2 = (s32[16]{0:T(128)S(1)}, s32[16]{0:T(128)}, u32[]{:S(2)}) copy-start(s32[16]{0:T(128)} %param.10) | copy-start | bytes 196
  131.5 29.5 %copy-start.1 = (s32[16]{0:T(128)S(1)}, s32[16]{0:T(128)}, u32[]{:S(2)}) copy-start(s32[16]{0:T(128)} %param.11) | copy-start | bytes 196
  133.6 27.0 %all-to-all-start = ((f32[64,1,64]{2,1,0:T(1,128)}), f32[64,1,64]{2,1,0:T(1,128)S(1)}, u32[]{:S(2)}, u32[]{:S(2)}) async-start(f32[64,1,64]{2,1,0:T(1,128)} %copy.21), calls=%async_computation | async-start | bytes 65536 | tf_op jit(solution)/shard_map/all_to_all | solution.py:36
Sparse Core Ops, SparseCore 0:
  23.2 99.6 all-gather.1
